TPU v7x, 32 devices: a whole 2x2x4 slice. The times are simulated.
32 devices in a mesh: groups: 2 (over y), ctx: 4 (over z), kv: 2 (over x), khalf: 2 (over core).
Axes of the slice: x: 2, y: 2, z: 4, core: 2. Of those that a mesh axis runs over, the one named last changes fastest.
Arguments:
- queries: bfloat16 [256, 8192], P(('groups', 'ctx'), 'kv'), parts along dimension 0, may hold values from -100 to 100
- cache_keys: bfloat16 [49152, 1024], P(('groups', 'ctx', 'khalf'), 'kv'), parts along dimension 0, may hold values from -7 to 7
- cache_values: bfloat16 [49152, 1024], P(('groups', 'ctx', 'khalf'), 'kv'), parts along dimension 0, may hold values from -6 to 6
- new_keys: bfloat16 [256, 1024], P(('groups', 'ctx'), 'kv'), parts along dimension 0, may hold values from -10 to 10
- new_values: bfloat16 [256, 1024], P(('groups', 'ctx'), 'kv'), parts along dimension 0, may hold values from -6 to 6
- cache_blocks: int32 [2], P('groups'), parts along dimension 0, may hold values from 48 to 192
- residual: bfloat16 [256, 8192], P('groups', ('ctx', 'khalf')), parts along dimension 0, may hold values from -20 to 20
- norm_gain: float32 [8192], P(('ctx', 'khalf')), may hold values from 0.1 to 1.9
- out_weight: bfloat16 [8192, 8192], P('kv', ('ctx', 'khalf')), may hold values from -0.0625 to 0.0625
- gate_up: bfloat16 [8192, 2, 14336], P(('ctx', 'khalf'), None, 'kv'), may hold values from -0.0625 to 0.0625
- down_weight: bfloat16 [14336, 8192], P('kv', ('ctx', 'khalf')), may hold values from -0.046875 to 0.046875
Outputs:
- layer_out: bfloat16 [256, 8192], P(('groups', 'kv'), ('ctx', 'khalf')), parts along dimension 0
There are 2 independent parts, one for each index of `groups`. A program takes and returns all parts, laid end to end along the dimension named above; an argument that names none is the same for every part. Nothing has to cross between parts.
Inputs may be any that keep to these rules, and one draw needn't show every extreme that they name: The first 128 * cache_blocks[0] cached positions are valid.
All inputs are finite; a program needn't handle non-finite values.
Results may differ from a plain program's by a relative error of at most 0.019.
Values may be sent and summed in bfloat16 or wider, within the bound.
No kernel may reach another device: no remote copies, remote signals or barrier semaphores. Data moves between devices by JAX's collectives and lax.ppermute only.
A program may use at most 128 MiB of HBM per device.

v0:
```python
import jax
import jax.numpy as jnp
from jax import lax
from jax.sharding import PartitionSpec as P

D = 8192
HQ = 64
KVH = 8
DH = 128
BLOCK = 128
NEG = -1e30
EPSILON = 1e-05


def shifted(value, axis, by):
    devices = lax.axis_size(axis)
    return lax.ppermute(value, axis, [(i, (i + by) % devices) for i in range(devices)])


def merged_2(value, axis, combine):
    everything = jax.tree.map(
        lambda part, kind: lax.all_gather(part.astype(kind), axis),
        value,
        jax.tree.map(lambda a: jnp.bfloat16 if a.dtype == jnp.float32 else a.dtype, value),
    )

    def take(k):
        return jax.tree.map(lambda part, own: part[k].astype(own.dtype), everything, value)

    return lax.fori_loop(
        1, lax.axis_size(axis), lambda k, so_far: combine(so_far, take(k)), take(0)
    )


def attend(query_block, key_block, value_block, allowed):
    row_count, local_groups, group_size, head_width = query_block.shape
    key_count = key_block.shape[0]
    keyed = key_block.reshape(key_count, local_groups, head_width)
    valued = value_block.reshape(key_count, local_groups, head_width)
    scores = jnp.einsum(
        "rkgd,nkd->rkgn", query_block, keyed, preferred_element_type=jnp.float32
    ) * head_width ** (-0.5)
    usable = allowed[:, None, None, :]
    scores = jnp.where(usable, scores, NEG)
    peak_score = jnp.max(scores, axis=3)
    weights = jnp.where(usable, jnp.exp(scores - peak_score[..., None]), 0.0)
    weight_sum = jnp.sum(weights, axis=3)
    summed = jnp.einsum(
        "rkgn,nkd->rkgd", weights.astype(jnp.bfloat16), valued, preferred_element_type=jnp.float32
    )
    return (summed, peak_score, weight_sum)


def combine(earlier_part, later_part):
    earlier_sum, earlier_peak, earlier_total = earlier_part
    later_sum, later_peak, later_total = later_part
    new_peak = jnp.maximum(earlier_peak, later_peak)
    earlier_scale = jnp.exp(earlier_peak - new_peak)
    later_scale = jnp.exp(later_peak - new_peak)
    return (
        earlier_sum * earlier_scale[..., None] + later_sum * later_scale[..., None],
        new_peak,
        earlier_total * earlier_scale + later_total * later_scale,
    )


def normalize(hidden_state, norm_gain):
    values32 = hidden_state.astype(jnp.float32)
    squares = lax.psum(jnp.sum(values32 * values32, axis=1), ("ctx", "khalf"))
    factor = lax.rsqrt(squares / D + EPSILON)
    return (values32 * factor[:, None] * norm_gain).astype(jnp.bfloat16)


def on_device(
    queries,
    cache_keys,
    cache_values,
    new_keys,
    new_values,
    cache_blocks,
    residual,
    norm_gain,
    out_weight,
    gate_up,
    down_weight,
):
    query_rows = queries.shape[0]
    group_size = HQ // KVH
    local_groups = cache_keys.shape[1] // DH
    local_queries = queries.reshape(query_rows, local_groups, group_size, DH)
    cache_length = cache_keys.shape[0]
    shard_index = lax.axis_index("ctx") * lax.axis_size("khalf") + lax.axis_index("khalf")
    positions = shard_index * cache_length + jnp.arange(cache_length, dtype=jnp.int32)
    cache_allowed = (positions < cache_blocks[0] * BLOCK)[None, :]
    query_start = lax.axis_index("ctx") * query_rows
    query_positions = query_start + jnp.arange(query_rows, dtype=jnp.int32)
    empty = (
        jnp.zeros((query_rows, local_groups, group_size, DH), jnp.float32),
        jnp.full((query_rows, local_groups, group_size), NEG, jnp.float32),
        jnp.zeros((query_rows, local_groups, group_size), jnp.float32),
    )

    def cycle_step(step_index, state_carry):
        visiting, partial_state = state_carry
        fresh = attend(visiting, cache_keys, cache_values, cache_allowed)
        partial_state = combine(partial_state, fresh)
        visiting = shifted(visiting, "ctx", 1)
        partial_state = (
            shifted(partial_state[0].astype(jnp.bfloat16), "ctx", 1).astype(jnp.float32),
            shifted(partial_state[1].astype(jnp.bfloat16), "ctx", 1).astype(jnp.float32),
            shifted(partial_state[2].astype(jnp.bfloat16), "ctx", 1).astype(jnp.float32),
        )
        return (visiting, partial_state)

    returned, cache_part = lax.fori_loop(
        0, lax.axis_size("ctx"), cycle_step, (local_queries, empty)
    )
    merged = merged_2(cache_part, "khalf", combine)
    piece_keys = lax.all_gather(new_keys, "ctx", axis=0, tiled=True)
    piece_values = lax.all_gather(new_values, "ctx", axis=0, tiled=True)
    key_positions = jnp.arange(piece_keys.shape[0], dtype=jnp.int32)
    allowed = key_positions[None, :] <= query_positions[:, None]
    own_part = combine(empty, attend(local_queries, piece_keys, piece_values, allowed))
    joined = combine(merged, own_part)
    attention = (
        (joined[0] / joined[2][..., None])
        .astype(jnp.bfloat16)
        .reshape(query_rows, local_groups * group_size * DH)
    )
    partial_rows = jnp.dot(
        lax.all_gather(attention, "ctx", axis=0, tiled=True),
        out_weight,
        preferred_element_type=jnp.float32,
    )
    projected = lax.psum(partial_rows.astype(jnp.bfloat16), "kv").astype(jnp.float32)
    hidden_state = (residual.astype(jnp.float32) + projected).astype(jnp.bfloat16)
    normed = normalize(hidden_state, norm_gain)
    own_rows = hidden_state.shape[0] // lax.axis_size("kv")
    kept = lax.dynamic_slice_in_dim(hidden_state, lax.axis_index("kv") * own_rows, own_rows, 0)
    local_width = gate_up.shape[0]
    local_hidden = gate_up.shape[2]
    merged_weight = gate_up.reshape(local_width, 2 * local_hidden)
    both = lax.psum_scatter(
        jnp.dot(normed, merged_weight, preferred_element_type=jnp.float32).astype(jnp.bfloat16),
        ("ctx", "khalf"),
        scatter_dimension=0,
        tiled=True,
    ).astype(jnp.float32)
    activated = (jax.nn.silu(both[:, :local_hidden]) * both[:, local_hidden:]).astype(jnp.bfloat16)
    partial_out = jnp.dot(
        lax.all_gather(activated, ("ctx", "khalf"), axis=0, tiled=True),
        down_weight,
        preferred_element_type=jnp.float32,
    )
    down = lax.psum_scatter(
        partial_out.astype(jnp.bfloat16), "kv", scatter_dimension=0, tiled=True
    ).astype(jnp.float32)
    return (kept.astype(jnp.float32) + down).astype(jnp.bfloat16)


def solution(mesh):
    in_specs = (
        P(("groups", "ctx"), "kv"),
        P(("groups", "ctx", "khalf"), "kv"),
        P(("groups", "ctx", "khalf"), "kv"),
        P(("groups", "ctx"), "kv"),
        P(("groups", "ctx"), "kv"),
        P("groups"),
        P("groups", ("ctx", "khalf")),
        P(("ctx", "khalf")),
        P("kv", ("ctx", "khalf")),
        P(("ctx", "khalf"), None, "kv"),
        P("kv", ("ctx", "khalf")),
    )
    out_specs = P(("groups", "kv"), ("ctx", "khalf"))
    return jax.shard_map(
        on_device, mesh=mesh, in_specs=in_specs, out_specs=out_specs, check_vma=False
    )
```

profile of v0, /device:TPU:0, one launch (start us, length us, event | category | flops | bytes accessed | tf_op | source)
XLA Modules:
  0.0 343.9 jit_solution(14457301337090552789)
XLA Ops:
  7.3 15.3 %all_gather.34 = bf16[128,512]{1,0:T(8,128)(2,1)S(1)} all-gather(bf16[32,512]{1,0:T(8,128)(2,1)} %param.16), channel_id=1, replica_groups=mesh['groups'=2,'ctx'=4,'kv'=2,'khalf'=2] {'ctx'}, dimensions={0}, use_global_device_ids=true | all-gather | bytes 163840 | tf_op jit(solution)/shard_map/all_gather | solution.py:119
  22.6 0.1 copy.99
  22.7 13.7 %all_gather.35 = bf16[128,512]{1,0:T(8,128)(2,1)S(1)} all-gather(bf16[32,512]{1,0:T(8,128)(2,1)} %param.17), channel_id=1, replica_groups=mesh['groups'=2,'ctx'=4,'kv'=2,'khalf'=2] {'ctx'}, dimensions={0}, use_global_device_ids=true | all-gather | bytes 163840 | tf_op jit(solution)/shard_map/all_gather | solution.py:120
  36.4 0.1 copy.104
  36.5 1.0 copy.130
  37.5 0.1 copy.92
  37.7 5.5 %reshape.182 = bf16[3072,4,128]{2,1,0:T(4,128)(2,1)} reshape(bf16[3072,512]{1,0:T(8,128)(2,1)} %param.14) | data formatting | bytes 6291456 | tf_op jit(solution)/shard_map/while/body/eval_jaxpr/reshape | solution.py:38
  43.2 5.5 %reshape.181 = bf16[3072,4,128]{2,1,0:T(4,128)(2,1)} reshape(bf16[3072,512]{1,0:T(8,128)(2,1)} %param.15) | data formatting | bytes 6291456 | tf_op jit(solution)/shard_map/while/body/eval_jaxpr/reshape | solution.py:39
  48.7 100.1 %while.4 = (s32[]{:T(128)}, bf16[32,4,8,128]{3,0,2,1:T(8,128)(2,1)S(1)}, f32[32,4,8,128]{3,0,2,1:T(8,128)S(1)}, f32[32,4,8]{0,2,1:T(8,128)S(1)}, f32[32,4,8]{0,2...) while((s32[]{:T(128)}, ...), condition=%wide.wide.region_3.4_spmd.clone, body=%wide.wide.region_0.3_spmd.clone.sunk | while | flops 1652313088 | bytes 48599340 | solution.py:115
  48.7 4.4 %bitcast_reduce_fusion.3 = (f32[32,4,8]{0,2,1:T(8,128)S(1)}, f32[4,3072,32,8]{1,2,3,0:T(8,128)S(1)}) fusion(pred[3072]{0:T(1024)(128)(4,1)S(1)} %add_compare_fusion.3, bf16[32,4,8,128]{3,0,2,1:T(8,128)(2,1)S(1)} %copy.169, bf16[3072,4,128,1]{2,1,0,3:T(4,128)(2,1)} %bitcast.100), kind=kOutput, calls=%fused_computation.2.clone.clone.1 | convolution fusion | flops 814742528 | bytes 15997952 | tf_op jit(solution)/shard_map/while/body/eval_jaxpr/rkgd,nkd->rkgn/dot_general | solution.py:40
  53.2 3.6 %fusion.100 = f32[32,4,8]{0,2,1:T(8,128)S(1)} fusion(f32[4,3072,32,8]{1,2,3,0:T(8,128)S(1)} %get-tuple-element.298, f32[32,4,8]{0,2,1:T(8,128)S(1)} %get-tuple-element.299, pred[3072]{0:T(1024)(128)(4,1)S(1)} %add_compare_fusion.3), kind=kLoop, calls=%fused_computation.6.clone.clone.1 | loop fusion | flops 15727616 | bytes 12594176 | tf_op jit(solution)/shard_map/while/body/eval_jaxpr/reduce_sum | solution.py:47
  56.8 5.6 %fusion.102 = bf16[32,4,8,128]{3,0,2,1:T(8,128)(2,1)S(1)} fusion(bf16[3072,4,128,1]{2,1,0,3:T(4,128)(2,1)} %bitcast.101, f32[4,3072,32,8]{1,2,3,0:T(8,128)S(1)} %get-tuple-element.298, f32[32,4,8]{0,2,1:T(8,128)S(1)} %get-tuple-element.299, pred[3072]{0:T(1024)(128)(4,1)S(1)} %add_compare_fusion.3, ...), kind=kOutput, calls=%fused_computation.17.clone.clone.1 | convolution fusion | flops 821690368 | bytes 16530433 | tf_op jit(solution)/shard_map/while/body/eval_jaxpr/rkgn,nkd->rkgd/dot_general | solution.py:48
  62.4 1.8 collective-permute-start.1
  64.2 2.9 collective-permute-start.2
  67.2 0.3 collective-permute-start.3
  67.4 6.1 %collective-permute-done.2 = bf16[32,4,8]{0,2,1:T(8,128)(2,1)S(1)} collective-permute-done((bf16[32,4,8]{0,2,1:T(8,128)(2,1)S(1)}, bf16[32,4,8]{0,2,1:T(8,128)(2,1)S(1)}, u32[]{:S(2)}, u32[]{:S(2)}) %collective-permute-start.2) | collective-permute-done | bytes 2080 | tf_op jit(solution)/shard_map/while/body/eval_jaxpr/ppermute | solution.py:17
  73.7 4.4 %bitcast_reduce_fusion.3 = (f32[32,4,8]{0,2,1:T(8,128)S(1)}, f32[4,3072,32,8]{1,2,3,0:T(8,128)S(1)}) fusion(pred[3072]{0:T(1024)(128)(4,1)S(1)} %add_compare_fusion.3, bf16[32,4,8,128]{3,0,2,1:T(8,128)(2,1)S(1)} %copy.169, bf16[3072,4,128,1]{2,1,0,3:T(4,128)(2,1)} %bitcast.100), kind=kOutput, calls=%fused_computation.2.clone.clone.1 | convolution fusion | flops 814742528 | bytes 15997952 | tf_op jit(solution)/shard_map/while/body/eval_jaxpr/rkgd,nkd->rkgn/dot_general | solution.py:40
  78.2 3.6 %fusion.100 = f32[32,4,8]{0,2,1:T(8,128)S(1)} fusion(f32[4,3072,32,8]{1,2,3,0:T(8,128)S(1)} %get-tuple-element.298, f32[32,4,8]{0,2,1:T(8,128)S(1)} %get-tuple-element.299, pred[3072]{0:T(1024)(128)(4,1)S(1)} %add_compare_fusion.3), kind=kLoop, calls=%fused_computation.6.clone.clone.1 | loop fusion | flops 15727616 | bytes 12594176 | tf_op jit(solution)/shard_map/while/body/eval_jaxpr/reduce_sum | solution.py:47
  81.8 5.6 %fusion.102 = bf16[32,4,8,128]{3,0,2,1:T(8,128)(2,1)S(1)} fusion(bf16[3072,4,128,1]{2,1,0,3:T(4,128)(2,1)} %bitcast.101, f32[4,3072,32,8]{1,2,3,0:T(8,128)S(1)} %get-tuple-element.298, f32[32,4,8]{0,2,1:T(8,128)S(1)} %get-tuple-element.299, pred[3072]{0:T(1024)(128)(4,1)S(1)} %add_compare_fusion.3, ...), kind=kOutput, calls=%fused_computation.17.clone.clone.1 | convolution fusion | flops 821690368 | bytes 16530433 | tf_op jit(solution)/shard_map/while/body/eval_jaxpr/rkgn,nkd->rkgd/dot_general | solution.py:48
  87.5 0.4 collective-permute-start
  87.9 2.5 collective-permute-start.2
  90.4 2.0 collective-permute-start.3
  92.4 6.1 %collective-permute-done.2 = bf16[32,4,8]{0,2,1:T(8,128)(2,1)S(1)} collective-permute-done((bf16[32,4,8]{0,2,1:T(8,128)(2,1)S(1)}, bf16[32,4,8]{0,2,1:T(8,128)(2,1)S(1)}, u32[]{:S(2)}, u32[]{:S(2)}) %collective-permute-start.2) | collective-permute-done | bytes 2080 | tf_op jit(solution)/shard_map/while/body/eval_jaxpr/ppermute | solution.py:17
  98.8 4.4 %bitcast_reduce_fusion.3 = (f32[32,4,8]{0,2,1:T(8,128)S(1)}, f32[4,3072,32,8]{1,2,3,0:T(8,128)S(1)}) fusion(pred[3072]{0:T(1024)(128)(4,1)S(1)} %add_compare_fusion.3, bf16[32,4,8,128]{3,0,2,1:T(8,128)(2,1)S(1)} %copy.169, bf16[3072,4,128,1]{2,1,0,3:T(4,128)(2,1)} %bitcast.100), kind=kOutput, calls=%fused_computation.2.clone.clone.1 | convolution fusion | flops 814742528 | bytes 15997952 | tf_op jit(solution)/shard_map/while/body/eval_jaxpr/rkgd,nkd->rkgn/dot_general | solution.py:40
  103.2 3.6 %fusion.100 = f32[32,4,8]{0,2,1:T(8,128)S(1)} fusion(f32[4,3072,32,8]{1,2,3,0:T(8,128)S(1)} %get-tuple-element.298, f32[32,4,8]{0,2,1:T(8,128)S(1)} %get-tuple-element.299, pred[3072]{0:T(1024)(128)(4,1)S(1)} %add_compare_fusion.3), kind=kLoop, calls=%fused_computation.6.clone.clone.1 | loop fusion | flops 15727616 | bytes 12594176 | tf_op jit(solution)/shard_map/while/body/eval_jaxpr/reduce_sum | solution.py:47
  106.8 5.6 %fusion.102 = bf16[32,4,8,128]{3,0,2,1:T(8,128)(2,1)S(1)} fusion(bf16[3072,4,128,1]{2,1,0,3:T(4,128)(2,1)} %bitcast.101, f32[4,3072,32,8]{1,2,3,0:T(8,128)S(1)} %get-tuple-element.298, f32[32,4,8]{0,2,1:T(8,128)S(1)} %get-tuple-element.299, pred[3072]{0:T(1024)(128)(4,1)S(1)} %add_compare_fusion.3, ...), kind=kOutput, calls=%fused_computation.17.clone.clone.1 | convolution fusion | flops 821690368 | bytes 16530433 | tf_op jit(solution)/shard_map/while/body/eval_jaxpr/rkgn,nkd->rkgd/dot_general | solution.py:48
  112.6 1.0 collective-permute-start.2
  113.6 3.8 %collective-permute-start.3 = (bf16[32,4,8]{0,2,1:T(8,128)(2,1)S(1)}, bf16[32,4,8]{0,2,1:T(8,128)(2,1)S(1)}, u32[]{:S(2)}, u32[]{:S(2)}) collective-permute-start(bf16[32,4,8]{0,2,1:T(8,128)(2,1)S(1)} %get-tuple-element.302), channel_id=1, source_target_pairs={{0,4},{4,8},{8,12},{12,0},{1,5},{5,9},{9,13},{13,1},{2,6},{6,10},{... | collective-permute-start | bytes 6152 | tf_op jit(solution)/shard_map/while/body/eval_jaxpr/ppermute | solution.py:17
  117.4 6.1 %collective-permute-done.2 = bf16[32,4,8]{0,2,1:T(8,128)(2,1)S(1)} collective-permute-done((bf16[32,4,8]{0,2,1:T(8,128)(2,1)S(1)}, bf16[32,4,8]{0,2,1:T(8,128)(2,1)S(1)}, u32[]{:S(2)}, u32[]{:S(2)}) %collective-permute-start.2) | collective-permute-done | bytes 2080 | tf_op jit(solution)/shard_map/while/body/eval_jaxpr/ppermute | solution.py:17
  123.8 4.4 %bitcast_reduce_fusion.3 = (f32[32,4,8]{0,2,1:T(8,128)S(1)}, f32[4,3072,32,8]{1,2,3,0:T(8,128)S(1)}) fusion(pred[3072]{0:T(1024)(128)(4,1)S(1)} %add_compare_fusion.3, bf16[32,4,8,128]{3,0,2,1:T(8,128)(2,1)S(1)} %copy.169, bf16[3072,4,128,1]{2,1,0,3:T(4,128)(2,1)} %bitcast.100), kind=kOutput, calls=%fused_computation.2.clone.clone.1 | convolution fusion | flops 814742528 | bytes 15997952 | tf_op jit(solution)/shard_map/while/body/eval_jaxpr/rkgd,nkd->rkgn/dot_general | solution.py:40
  128.2 3.6 %fusion.100 = f32[32,4,8]{0,2,1:T(8,128)S(1)} fusion(f32[4,3072,32,8]{1,2,3,0:T(8,128)S(1)} %get-tuple-element.298, f32[32,4,8]{0,2,1:T(8,128)S(1)} %get-tuple-element.299, pred[3072]{0:T(1024)(128)(4,1)S(1)} %add_compare_fusion.3), kind=kLoop, calls=%fused_computation.6.clone.clone.1 | loop fusion | flops 15727616 | bytes 12594176 | tf_op jit(solution)/shard_map/while/body/eval_jaxpr/reduce_sum | solution.py:47
  131.8 5.6 %fusion.102 = bf16[32,4,8,128]{3,0,2,1:T(8,128)(2,1)S(1)} fusion(bf16[3072,4,128,1]{2,1,0,3:T(4,128)(2,1)} %bitcast.101, f32[4,3072,32,8]{1,2,3,0:T(8,128)S(1)} %get-tuple-element.298, f32[32,4,8]{0,2,1:T(8,128)S(1)} %get-tuple-element.299, pred[3072]{0:T(1024)(128)(4,1)S(1)} %add_compare_fusion.3, ...), kind=kOutput, calls=%fused_computation.17.clone.clone.1 | convolution fusion | flops 821690368 | bytes 16530433 | tf_op jit(solution)/shard_map/while/body/eval_jaxpr/rkgn,nkd->rkgd/dot_general | solution.py:48
  137.6 0.6 collective-permute-start.2
  138.2 4.3 %collective-permute-start.3 = (bf16[32,4,8]{0,2,1:T(8,128)(2,1)S(1)}, bf16[32,4,8]{0,2,1:T(8,128)(2,1)S(1)}, u32[]{:S(2)}, u32[]{:S(2)}) collective-permute-start(bf16[32,4,8]{0,2,1:T(8,128)(2,1)S(1)} %get-tuple-element.302), channel_id=1, source_target_pairs={{0,4},{4,8},{8,12},{12,0},{1,5},{5,9},{9,13},{13,1},{2,6},{6,10},{... | collective-permute-start | bytes 6152 | tf_op jit(solution)/shard_map/while/body/eval_jaxpr/ppermute | solution.py:17
  142.5 6.1 %collective-permute-done.2 = bf16[32,4,8]{0,2,1:T(8,128)(2,1)S(1)} collective-permute-done((bf16[32,4,8]{0,2,1:T(8,128)(2,1)S(1)}, bf16[32,4,8]{0,2,1:T(8,128)(2,1)S(1)}, u32[]{:S(2)}, u32[]{:S(2)}) %collective-permute-start.2) | collective-permute-done | bytes 2080 | tf_op jit(solution)/shard_map/while/body/eval_jaxpr/ppermute | solution.py:17
  148.8 0.1 copy.109
  148.9 0.1 copy.94
  149.0 1.9 all-gather.1
  150.9 0.1 copy.127
  151.0 0.1 copy.126
  151.0 1.8 all-gather.2
  152.9 0.1 copy.128
  153.0 0.1 copy.129
  153.1 0.4 fusion.74
  153.5 0.4 fusion.53
  154.5 0.3 copy.151
  154.8 2.2 all-gather
  157.0 1.1 fusion.46
  158.2 0.8 copy.156
  159.0 26.3 %all-gather.6.cloned.1.call-done = bf16[128,4096]{1,0:T(8,128)(2,1)} async-done(((bf16[32,4096]{1,0:T(8,128)(2,1)}), bf16[128,4096]{1,0:T(8,128)(2,1)}) %all-gather.6.cloned.1.call-update) | async-done | bytes 1048592 | tf_op jit(solution)/shard_map/all_gather | solution.py:131
  185.3 5.7 %convolution_convert_fusion.1 = bf16[128,1024]{1,0:T(8,128)(2,1)} fusion(bf16[128,4096]{1,0:T(8,128)(2,1)} %all-gather.6.cloned.1.call-done, bf16[4096,1024]{1,0:T(8,128)(2,1)} %param.21), kind=kOutput, calls=%fused_computation.40 | convolution fusion | flops 1073872896 | bytes 9699328 | tf_op jit(solution)/shard_map/dot_general | solution.py:130
  191.1 0.2 reduce-scatter.3.cloned.1.call-start
  191.3 20.5 %copy.132 = bf16[128,8,2,7168]{3,1,2,0:T(8,128)(2,1)} copy(bf16[128,8,2,7168]{3,2,1,0:T(2,128)(2,1)} %bitcast.99) | data formatting | bytes 58720256
  211.9 2.0 all-reduce.2.cloned.1.call-done
  213.9 1.1 fusion.47
  215.0 15.8 %psum.15 = f32[128]{0:T(128)S(1)} all-reduce(f32[128]{0:T(128)S(1)} %get-tuple-element.167), channel_id=1, replica_groups=mesh['groups'=2,'ctx'=4,'kv'=2,'khalf'=2] {'ctx','khalf'}, use_global_device_ids=true, to_apply=%region_8.9 | all-reduce | flops 128 | bytes 1024 | tf_op jit(solution)/shard_map/psum | solution.py:69
  230.9 15.2 %convolution_convert_fusion = bf16[128,14336]{1,0:T(8,128)(2,1)} fusion(bf16[1024,14336]{1,0:T(8,128)(2,1)} %bitcast.98, bf16[128,1024]{1,0:T(8,128)(2,1)S(1)} %get-tuple-element.168, f32[1024]{0:T(1024)S(1)} %copy-done.1, f32[128]{0:T(128)S(1)} %add_rsqrt_fusion), kind=kOutput, calls=%fused_computation.30 | convolution fusion | flops 3760455680 | bytes 33296896 | tf_op jit(solution)/shard_map/dot_general | solution.py:144
  246.1 42.3 %reduce-scatter.3.cloned.1.call-done = bf16[16,14336]{1,0:T(8,128)(2,1)} async-done(((bf16[128,14336]{1,0:T(8,128)(2,1)}), bf16[16,14336]{1,0:T(8,128)(2,1)}) %reduce-scatter.3.cloned.1.call-update) | async-done | bytes 458768 | tf_op jit(solution)/shard_map/reduce_scatter | solution.py:143
  288.4 1.1 convert_element_type.179
  289.5 0.8 fusion.52
  290.4 25.5 %all-gather.8.cloned.1.call-done = bf16[128,7168]{1,0:T(8,128)(2,1)} async-done(((bf16[16,7168]{1,0:T(8,128)(2,1)}), bf16[128,7168]{1,0:T(8,128)(2,1)}) %all-gather.8.cloned.1.call-update) | async-done | bytes 1835024 | tf_op jit(solution)/shard_map/all_gather | solution.py:151
  315.9 8.5 %convolution_convert_fusion.2 = bf16[128,1024]{1,0:T(8,128)(2,1)} fusion(bf16[128,7168]{1,0:T(8,128)(2,1)} %all-gather.8.cloned.1.call-done, bf16[7168,1024]{1,0:T(8,128)(2,1)} %param.23), kind=kOutput, calls=%fused_computation.42 | convolution fusion | flops 1879179264 | bytes 16777216 | tf_op jit(solution)/shard_map/dot_general | solution.py:150
  324.4 11.3 %reduce-scatter.5.cloned.1.call-done = bf16[64,1024]{1,0:T(8,128)(2,1)} async-done(((bf16[128,1024]{1,0:T(8,128)(2,1)}), bf16[64,1024]{1,0:T(8,128)(2,1)}) %reduce-scatter.5.cloned.1.call-update) | async-done | bytes 131088 | tf_op jit(solution)/shard_map/reduce_scatter | solution.py:155
  335.8 1.6 add_convert_fusion.1
  (78 shorter events, 2.2 us)
Async XLA Ops:
  6.5 178.8 %all-gather.6.cloned.1.call-start = ((), (), s32[]{:S(2)}) async-start(), calls=%async_computation.2 | async-start | bytes 1310720 | tf_op jit(solution)/shard_map/all_gather | solution.py:131
  62.4 11.2 %collective-permute-start.1 = (bf16[32,4,8,128]{3,0,2,1:T(8,128)(2,1)S(1)}, bf16[32,4,8,128]{3,0,2,1:T(8,128)(2,1)S(1)}, u32[]{:S(2)}, u32[]{:S(2)}) collective-permute-start(bf16[32,4,8,128]{3,0,2,1:T(8,128)(2,1)S(1)} %fusion.102), channel_id=1, source_target_pairs={{0,4},{4,8},{8,12},{12,0},{1,5},{5,9},{9,13},{13,1},{2,6},{6,10},{... | collective-permute-start | bytes 786440 | tf_op jit(solution)/shard_map/while/body/eval_jaxpr/ppermute | solution.py:17
  64.2 9.5 %collective-permute-start = (bf16[32,4,8,128]{3,0,2,1:T(8,128)(2,1)S(1)}, bf16[32,4,8,128]{3,0,2,1:T(8,128)(2,1)S(1)}, u32[]{:S(2)}, u32[]{:S(2)}) collective-permute-start(bf16[32,4,8,128]{3,0,2,1:T(8,128)(2,1)S(1)} %copy.169), channel_id=1, source_target_pairs={{0,4},{4,8},{8,12},{12,0},{1,5},{5,9},{9,13},{13,1},{2,6},{6,10},{... | collective-permute-start | bytes 786440 | tf_op jit(solution)/shard_map/while/body/eval_jaxpr/ppermute | solution.py:17
  64.2 9.3 %collective-permute-start.2 = (bf16[32,4,8]{0,2,1:T(8,128)(2,1)S(1)}, bf16[32,4,8]{0,2,1:T(8,128)(2,1)S(1)}, u32[]{:S(2)}, u32[]{:S(2)}) collective-permute-start(bf16[32,4,8]{0,2,1:T(8,128)(2,1)S(1)} %fusion.103), channel_id=1, source_target_pairs={{0,4},{4,8},{8,12},{12,0},{1,5},{5,9},{9,13},{13,1},{2,6},{6,10},{... | collective-permute-start | bytes 6152 | tf_op jit(solution)/shard_map/while/body/eval_jaxpr/ppermute | solution.py:17
  67.2 6.4 %collective-permute-start.3 = (bf16[32,4,8]{0,2,1:T(8,128)(2,1)S(1)}, bf16[32,4,8]{0,2,1:T(8,128)(2,1)S(1)}, u32[]{:S(2)}, u32[]{:S(2)}) collective-permute-start(bf16[32,4,8]{0,2,1:T(8,128)(2,1)S(1)} %get-tuple-element.302), channel_id=1, source_target_pairs={{0,4},{4,8},{8,12},{12,0},{1,5},{5,9},{9,13},{13,1},{2,6},{6,10},{... | collective-permute-start | bytes 6152 | tf_op jit(solution)/shard_map/while/body/eval_jaxpr/ppermute | solution.py:17
  87.4 11.2 %collective-permute-start.1 = (bf16[32,4,8,128]{3,0,2,1:T(8,128)(2,1)S(1)}, bf16[32,4,8,128]{3,0,2,1:T(8,128)(2,1)S(1)}, u32[]{:S(2)}, u32[]{:S(2)}) collective-permute-start(bf16[32,4,8,128]{3,0,2,1:T(8,128)(2,1)S(1)} %fusion.102), channel_id=1, source_target_pairs={{0,4},{4,8},{8,12},{12,0},{1,5},{5,9},{9,13},{13,1},{2,6},{6,10},{... | collective-permute-start | bytes 786440 | tf_op jit(solution)/shard_map/while/body/eval_jaxpr/ppermute | solution.py:17
  87.5 11.2 %collective-permute-start = (bf16[32,4,8,128]{3,0,2,1:T(8,128)(2,1)S(1)}, bf16[32,4,8,128]{3,0,2,1:T(8,128)(2,1)S(1)}, u32[]{:S(2)}, u32[]{:S(2)}) collective-permute-start(bf16[32,4,8,128]{3,0,2,1:T(8,128)(2,1)S(1)} %copy.169), channel_id=1, source_target_pairs={{0,4},{4,8},{8,12},{12,0},{1,5},{5,9},{9,13},{13,1},{2,6},{6,10},{... | collective-permute-start | bytes 786440 | tf_op jit(solution)/shard_map/while/body/eval_jaxpr/ppermute | solution.py:17
  87.9 10.6 %collective-permute-start.2 = (bf16[32,4,8]{0,2,1:T(8,128)(2,1)S(1)}, bf16[32,4,8]{0,2,1:T(8,128)(2,1)S(1)}, u32[]{:S(2)}, u32[]{:S(2)}) collective-permute-start(bf16[32,4,8]{0,2,1:T(8,128)(2,1)S(1)} %fusion.103), channel_id=1, source_target_pairs={{0,4},{4,8},{8,12},{12,0},{1,5},{5,9},{9,13},{13,1},{2,6},{6,10},{... | collective-permute-start | bytes 6152 | tf_op jit(solution)/shard_map/while/body/eval_jaxpr/ppermute | solution.py:17
  90.4 8.2 %collective-permute-start.3 = (bf16[32,4,8]{0,2,1:T(8,128)(2,1)S(1)}, bf16[32,4,8]{0,2,1:T(8,128)(2,1)S(1)}, u32[]{:S(2)}, u32[]{:S(2)}) collective-permute-start(bf16[32,4,8]{0,2,1:T(8,128)(2,1)S(1)} %get-tuple-element.302), channel_id=1, source_target_pairs={{0,4},{4,8},{8,12},{12,0},{1,5},{5,9},{9,13},{13,1},{2,6},{6,10},{... | collective-permute-start | bytes 6152 | tf_op jit(solution)/shard_map/while/body/eval_jaxpr/ppermute | solution.py:17
  112.4 11.2 %collective-permute-start.1 = (bf16[32,4,8,128]{3,0,2,1:T(8,128)(2,1)S(1)}, bf16[32,4,8,128]{3,0,2,1:T(8,128)(2,1)S(1)}, u32[]{:S(2)}, u32[]{:S(2)}) collective-permute-start(bf16[32,4,8,128]{3,0,2,1:T(8,128)(2,1)S(1)} %fusion.102), channel_id=1, source_target_pairs={{0,4},{4,8},{8,12},{12,0},{1,5},{5,9},{9,13},{13,1},{2,6},{6,10},{... | collective-permute-start | bytes 786440 | tf_op jit(solution)/shard_map/while/body/eval_jaxpr/ppermute | solution.py:17
  112.5 11.2 %collective-permute-start = (bf16[32,4,8,128]{3,0,2,1:T(8,128)(2,1)S(1)}, bf16[32,4,8,128]{3,0,2,1:T(8,128)(2,1)S(1)}, u32[]{:S(2)}, u32[]{:S(2)}) collective-permute-start(bf16[32,4,8,128]{3,0,2,1:T(8,128)(2,1)S(1)} %copy.169), channel_id=1, source_target_pairs={{0,4},{4,8},{8,12},{12,0},{1,5},{5,9},{9,13},{13,1},{2,6},{6,10},{... | collective-permute-start | bytes 786440 | tf_op jit(solution)/shard_map/while/body/eval_jaxpr/ppermute | solution.py:17
  112.6 11.0 %collective-permute-start.2 = (bf16[32,4,8]{0,2,1:T(8,128)(2,1)S(1)}, bf16[32,4,8]{0,2,1:T(8,128)(2,1)S(1)}, u32[]{:S(2)}, u32[]{:S(2)}) collective-permute-start(bf16[32,4,8]{0,2,1:T(8,128)(2,1)S(1)} %fusion.103), channel_id=1, source_target_pairs={{0,4},{4,8},{8,12},{12,0},{1,5},{5,9},{9,13},{13,1},{2,6},{6,10},{... | collective-permute-start | bytes 6152 | tf_op jit(solution)/shard_map/while/body/eval_jaxpr/ppermute | solution.py:17
  113.6 10.0 %collective-permute-start.3 = (bf16[32,4,8]{0,2,1:T(8,128)(2,1)S(1)}, bf16[32,4,8]{0,2,1:T(8,128)(2,1)S(1)}, u32[]{:S(2)}, u32[]{:S(2)}) collective-permute-start(bf16[32,4,8]{0,2,1:T(8,128)(2,1)S(1)} %get-tuple-element.302), channel_id=1, source_target_pairs={{0,4},{4,8},{8,12},{12,0},{1,5},{5,9},{9,13},{13,1},{2,6},{6,10},{... | collective-permute-start | bytes 6152 | tf_op jit(solution)/shard_map/while/body/eval_jaxpr/ppermute | solution.py:17
  137.4 11.2 %collective-permute-start.1 = (bf16[32,4,8,128]{3,0,2,1:T(8,128)(2,1)S(1)}, bf16[32,4,8,128]{3,0,2,1:T(8,128)(2,1)S(1)}, u32[]{:S(2)}, u32[]{:S(2)}) collective-permute-start(bf16[32,4,8,128]{3,0,2,1:T(8,128)(2,1)S(1)} %fusion.102), channel_id=1, source_target_pairs={{0,4},{4,8},{8,12},{12,0},{1,5},{5,9},{9,13},{13,1},{2,6},{6,10},{... | collective-permute-start | bytes 786440 | tf_op jit(solution)/shard_map/while/body/eval_jaxpr/ppermute | solution.py:17
  137.5 11.2 %collective-permute-start = (bf16[32,4,8,128]{3,0,2,1:T(8,128)(2,1)S(1)}, bf16[32,4,8,128]{3,0,2,1:T(8,128)(2,1)S(1)}, u32[]{:S(2)}, u32[]{:S(2)}) collective-permute-start(bf16[32,4,8,128]{3,0,2,1:T(8,128)(2,1)S(1)} %copy.169), channel_id=1, source_target_pairs={{0,4},{4,8},{8,12},{12,0},{1,5},{5,9},{9,13},{13,1},{2,6},{6,10},{... | collective-permute-start | bytes 786440 | tf_op jit(solution)/shard_map/while/body/eval_jaxpr/ppermute | solution.py:17
  137.6 11.0 %collective-permute-start.2 = (bf16[32,4,8]{0,2,1:T(8,128)(2,1)S(1)}, bf16[32,4,8]{0,2,1:T(8,128)(2,1)S(1)}, u32[]{:S(2)}, u32[]{:S(2)}) collective-permute-start(bf16[32,4,8]{0,2,1:T(8,128)(2,1)S(1)} %fusion.103), channel_id=1, source_target_pairs={{0,4},{4,8},{8,12},{12,0},{1,5},{5,9},{9,13},{13,1},{2,6},{6,10},{... | collective-permute-start | bytes 6152 | tf_op jit(solution)/shard_map/while/body/eval_jaxpr/ppermute | solution.py:17
  138.2 10.5 %collective-permute-start.3 = (bf16[32,4,8]{0,2,1:T(8,128)(2,1)S(1)}, bf16[32,4,8]{0,2,1:T(8,128)(2,1)S(1)}, u32[]{:S(2)}, u32[]{:S(2)}) collective-permute-start(bf16[32,4,8]{0,2,1:T(8,128)(2,1)S(1)} %get-tuple-element.302), channel_id=1, source_target_pairs={{0,4},{4,8},{8,12},{12,0},{1,5},{5,9},{9,13},{13,1},{2,6},{6,10},{... | collective-permute-start | bytes 6152 | tf_op jit(solution)/shard_map/while/body/eval_jaxpr/ppermute | solution.py:17
  159.0 54.9 %all-reduce.2.cloned.1.call-start = ((), (), s32[]{:S(2)}) async-start(), calls=%async_computation.3 | async-start | bytes 524288 | tf_op jit(solution)/shard_map/psum | solution.py:135
  191.1 97.4 %reduce-scatter.3.cloned.1.call-start = ((), (), s32[]{:S(2)}) async-start(), calls=%async_computation.4 | async-start | bytes 4128768 | tf_op jit(solution)/shard_map/reduce_scatter | solution.py:143
  191.3 22.6 %copy-start = (bf16[128,1024]{1,0:T(8,128)(2,1)S(1)}, bf16[128,1024]{1,0:T(8,128)(2,1)}, u32[]{:S(2)}) copy-start(bf16[128,1024]{1,0:T(8,128)(2,1)} %param.19) | copy-start | bytes 786436
  191.3 39.6 %copy-start.1 = (f32[1024]{0:T(1024)S(1)}, f32[1024]{0:T(1024)}, u32[]{:S(2)}) copy-start(f32[1024]{0:T(1024)} %param.20) | copy-start | bytes 12292
  246.1 69.8 %all-gather.8.cloned.1.call-start = ((), (), s32[]{:S(2)}) async-start(), calls=%async_computation.5 | async-start | bytes 2064384 | tf_op jit(solution)/shard_map/all_gather | solution.py:151
  290.4 45.4 %reduce-scatter.5.cloned.1.call-start = ((), (), s32[]{:S(2)}) async-start(), calls=%async_computation.6 | async-start | bytes 393216 | tf_op jit(solution)/shard_map/reduce_scatter | solution.py:155
Sparse Core Ops, SparseCore 0:
  159.1 26.1 all-gather.5
  191.2 22.6 all-reduce.1
  246.2 42.2 reduce-scatter.2
  290.5 25.3 all-gather.7
  324.5 11.1 reduce-scatter.4
where the time goes:
time: 345 us; the launch traced here: 344 us
  waiting for transfers between devices  132 us (38%)
  matrix products  71.1 us (21%)
  blocking collectives  50.7 us (15%)
  local copies, waits for them, and re-layouts  35.3 us (10%)
  starting transfers between devices  20.3 us (6%)
  other arithmetic  19.8 us (6%)
  between operations  14 us (4%)
    reduce_scatter x1, waiting for transfers between devices, on_device(): lax.psum_scatter(jnp.dot(normed, merged_weight, preferred_element_type=jn...  42.3 us
    all_gather x1, waiting for transfers between devices, on_device(): lax.all_gather(attention, 'ctx', axis=0, tiled=True)  26.3 us
    all_gather x1, waiting for transfers between devices, on_device(): lax.all_gather(activated, ('ctx', 'khalf'), axis=0, tiled=True)  25.5 us
    ppermute x16, waiting for transfers between devices, shifted(): lax.ppermute(value, axis, [(i, (i + by) % devices) for i in range(devices)])  24.8 us
    dot_general x5, matrix products, attend(): jnp.einsum('rkgn,nkd->rkgd', weights.astype(jnp.bfloat16), valued, prefer...  23.6 us
    unnamed x12, local copies, waits for them, and re-layouts  22.8 us
    ppermute x16, starting transfers between devices, shifted(): lax.ppermute(value, axis, [(i, (i + by) % devices) for i in range(devices)])  20 us
    dot_general x5, matrix products, attend(): jnp.einsum('rkgd,nkd->rkgn', query_block, keyed, preferred_element_type=j...  18.1 us
  transfers between devices with their start and end apart: 21, of which 13 were waited for; matrix products, arithmetic and copies ran while one was open for 6% of the time, Pallas kernels for 0%

commit v1 on v0

--- a/solution.py
+++ b/solution.py
@@ -116,8 +116,11 @@
         0, lax.axis_size("ctx"), cycle_step, (local_queries, empty)
     )
     merged = merged_2(cache_part, "khalf", combine)
-    piece_keys = lax.all_gather(new_keys, "ctx", axis=0, tiled=True)
-    piece_values = lax.all_gather(new_values, "ctx", axis=0, tiled=True)
+    piece_keys, piece_values = jnp.split(
+        lax.all_gather(jnp.concatenate([new_keys, new_values], axis=1), "ctx", axis=0, tiled=True),
+        [new_keys.shape[1]],
+        axis=1,
+    )
     key_positions = jnp.arange(piece_keys.shape[0], dtype=jnp.int32)
     allowed = key_positions[None, :] <= query_positions[:, None]
     own_part = combine(empty, attend(local_queries, piece_keys, piece_values, allowed))

time: 345 us -> 338 us (0.980)
  blocking collectives: 50.7 us -> 37.4 us
  waiting for transfers between devices: 132 us -> 139 us
    all_gather x2 -> x1, blocking collectives: 29 us -> 15.6 us  [on_device(): lax.all_gather(jnp.concatenate([new_keys, new_values], axis=1), 'ctx', ax...]
    ppermute x16, waiting for transfers between devices: 24.8 us -> 31.1 us  [shifted(): lax.ppermute(value, axis, [(i, (i + by) % devices) for i in range(devices)])]
    unnamed x12 -> x14, local copies, waits for them, and re-layouts: 22.8 us -> 23.1 us
where the time goes in v1:
time: 338 us; the launch traced here: 337 us
  waiting for transfers between devices  139 us (41%)
  matrix products  71.3 us (21%)
  blocking collectives  37.4 us (11%)
  local copies, waits for them, and re-layouts  34.5 us (10%)
  other arithmetic  20.6 us (6%)
  starting transfers between devices  20.5 us (6%)
  between operations  14 us (4%)
    reduce_scatter x1, waiting for transfers between devices, on_device(): lax.psum_scatter(jnp.dot(normed, merged_weight, preferred_element_type=jn...  42.3 us
    ppermute x16, waiting for transfers between devices, shifted(): lax.ppermute(value, axis, [(i, (i + by) % devices) for i in range(devices)])  31.1 us
    all_gather x1, waiting for transfers between devices, on_device(): lax.all_gather(attention, 'ctx', axis=0, tiled=True)  26.3 us
    all_gather x1, waiting for transfers between devices, on_device(): lax.all_gather(activated, ('ctx', 'khalf'), axis=0, tiled=True)  25.5 us
    dot_general x5, matrix products, attend(): jnp.einsum('rkgn,nkd->rkgd', weights.astype(jnp.bfloat16), valued, prefer...  23.8 us
    unnamed x14, local copies, waits for them, and re-layouts  23.1 us
    ppermute x16, starting transfers between devices, shifted(): lax.ppermute(value, axis, [(i, (i + by) % devices) for i in range(devices)])  20.1 us
    dot_general x5, matrix products, attend(): jnp.einsum('rkgd,nkd->rkgn', query_block, keyed, preferred_element_type=j...  18.1 us
  transfers between devices with their start and end apart: 21, of which 13 were waited for; matrix products, arithmetic and copies ran while one was open for 6% of the time, Pallas kernels for 0%

profile of v1, /device:TPU:0, one launch (start us, length us, event | category | flops | bytes accessed | tf_op | source)
XLA Modules:
  0.0 337.2 jit_solution(6201715632840854290)
XLA Ops:
  7.3 0.8 pad_maximum_fusion
  8.1 15.6 %all_gather.31 = bf16[128,1024]{1,0:T(8,128)(2,1)S(1)} all-gather(bf16[32,1024]{1,0:T(8,128)(2,1)S(1)} %pad_maximum_fusion), channel_id=1, replica_groups=mesh['groups'=2,'ctx'=4,'kv'=2,'khalf'=2] {'ctx'}, dimensions={0}, use_global_device_ids=true | all-gather | bytes 327680 | tf_op jit(solution)/shard_map/all_gather | solution.py:120
  23.7 0.1 copy.94
  23.9 0.1 copy.95
  24.0 1.0 copy.98
  25.0 0.1 copy.67
  25.1 5.5 %reshape.182 = bf16[3072,4,128]{2,1,0:T(4,128)(2,1)} reshape(bf16[3072,512]{1,0:T(8,128)(2,1)} %param.14) | data formatting | bytes 6291456 | tf_op jit(solution)/shard_map/while/body/eval_jaxpr/reshape | solution.py:38
  30.6 5.5 %reshape.181 = bf16[3072,4,128]{2,1,0:T(4,128)(2,1)} reshape(bf16[3072,512]{1,0:T(8,128)(2,1)} %param.15) | data formatting | bytes 6291456 | tf_op jit(solution)/shard_map/while/body/eval_jaxpr/reshape | solution.py:39
  36.1 106.5 %while.4 = (s32[]{:T(128)}, bf16[32,4,8,128]{3,0,2,1:T(8,128)(2,1)S(1)}, f32[32,4,8,128]{3,0,2,1:T(8,128)S(1)}, f32[32,4,8]{0,2,1:T(8,128)S(1)}, f32[32,4,8]{0,2...) while((s32[]{:T(128)}, ...), condition=%wide.wide.region_3.4_spmd.clone, body=%wide.wide.region_0.3_spmd.clone.sunk | while | flops 1652313088 | bytes 48599340 | solution.py:115
  36.2 4.4 %bitcast_reduce_fusion.3 = (f32[32,4,8]{0,2,1:T(8,128)S(1)}, f32[4,3072,32,8]{1,2,3,0:T(8,128)S(1)}) fusion(pred[3072]{0:T(1024)(128)(4,1)S(1)} %add_compare_fusion.3, bf16[32,4,8,128]{3,0,2,1:T(8,128)(2,1)S(1)} %copy.133, bf16[3072,4,128,1]{2,1,0,3:T(4,128)(2,1)} %bitcast.100), kind=kOutput, calls=%fused_computation.2.clone.clone.1 | convolution fusion | flops 814742528 | bytes 15997952 | tf_op jit(solution)/shard_map/while/body/eval_jaxpr/rkgd,nkd->rkgn/dot_general | solution.py:40
  40.6 3.6 %fusion.105 = f32[32,4,8]{0,2,1:T(8,128)S(1)} fusion(f32[4,3072,32,8]{1,2,3,0:T(8,128)S(1)} %get-tuple-element.298, f32[32,4,8]{0,2,1:T(8,128)S(1)} %get-tuple-element.299, pred[3072]{0:T(1024)(128)(4,1)S(1)} %add_compare_fusion.3), kind=kLoop, calls=%fused_computation.6.clone.clone.1 | loop fusion | flops 15727616 | bytes 12594176 | tf_op jit(solution)/shard_map/while/body/eval_jaxpr/reduce_sum | solution.py:47
  44.2 5.6 %fusion.107 = bf16[32,4,8,128]{3,0,2,1:T(8,128)(2,1)S(1)} fusion(bf16[3072,4,128,1]{2,1,0,3:T(4,128)(2,1)} %bitcast.101, f32[4,3072,32,8]{1,2,3,0:T(8,128)S(1)} %get-tuple-element.298, f32[32,4,8]{0,2,1:T(8,128)S(1)} %get-tuple-element.299, pred[3072]{0:T(1024)(128)(4,1)S(1)} %add_compare_fusion.3, ...), kind=kOutput, calls=%fused_computation.17.clone.clone.1 | convolution fusion | flops 821690368 | bytes 16530433 | tf_op jit(solution)/shard_map/while/body/eval_jaxpr/rkgn,nkd->rkgd/dot_general | solution.py:48
  49.8 2.1 collective-permute-start.1
  52.0 2.9 collective-permute-start.2
  54.9 0.1 collective-permute-start.3
  55.0 8.9 %collective-permute-done.2 = bf16[32,4,8]{0,2,1:T(8,128)(2,1)S(1)} collective-permute-done((bf16[32,4,8]{0,2,1:T(8,128)(2,1)S(1)}, bf16[32,4,8]{0,2,1:T(8,128)(2,1)S(1)}, u32[]{:S(2)}, u32[]{:S(2)}) %collective-permute-start.2) | collective-permute-done | bytes 2080 | tf_op jit(solution)/shard_map/while/body/eval_jaxpr/ppermute | solution.py:17
  63.9 0.1 collective-permute-done.3
  64.1 4.4 %bitcast_reduce_fusion.3 = (f32[32,4,8]{0,2,1:T(8,128)S(1)}, f32[4,3072,32,8]{1,2,3,0:T(8,128)S(1)}) fusion(pred[3072]{0:T(1024)(128)(4,1)S(1)} %add_compare_fusion.3, bf16[32,4,8,128]{3,0,2,1:T(8,128)(2,1)S(1)} %copy.133, bf16[3072,4,128,1]{2,1,0,3:T(4,128)(2,1)} %bitcast.100), kind=kOutput, calls=%fused_computation.2.clone.clone.1 | convolution fusion | flops 814742528 | bytes 15997952 | tf_op jit(solution)/shard_map/while/body/eval_jaxpr/rkgd,nkd->rkgn/dot_general | solution.py:40
  68.6 3.6 %fusion.105 = f32[32,4,8]{0,2,1:T(8,128)S(1)} fusion(f32[4,3072,32,8]{1,2,3,0:T(8,128)S(1)} %get-tuple-element.298, f32[32,4,8]{0,2,1:T(8,128)S(1)} %get-tuple-element.299, pred[3072]{0:T(1024)(128)(4,1)S(1)} %add_compare_fusion.3), kind=kLoop, calls=%fused_computation.6.clone.clone.1 | loop fusion | flops 15727616 | bytes 12594176 | tf_op jit(solution)/shard_map/while/body/eval_jaxpr/reduce_sum | solution.py:47
  72.2 5.6 %fusion.107 = bf16[32,4,8,128]{3,0,2,1:T(8,128)(2,1)S(1)} fusion(bf16[3072,4,128,1]{2,1,0,3:T(4,128)(2,1)} %bitcast.101, f32[4,3072,32,8]{1,2,3,0:T(8,128)S(1)} %get-tuple-element.298, f32[32,4,8]{0,2,1:T(8,128)S(1)} %get-tuple-element.299, pred[3072]{0:T(1024)(128)(4,1)S(1)} %add_compare_fusion.3, ...), kind=kOutput, calls=%fused_computation.17.clone.clone.1 | convolution fusion | flops 821690368 | bytes 16530433 | tf_op jit(solution)/shard_map/while/body/eval_jaxpr/rkgn,nkd->rkgd/dot_general | solution.py:48
  78.0 1.4 collective-permute-start.2
  79.3 3.5 %collective-permute-start.3 = (bf16[32,4,8]{0,2,1:T(8,128)(2,1)S(1)}, bf16[32,4,8]{0,2,1:T(8,128)(2,1)S(1)}, u32[]{:S(2)}, u32[]{:S(2)}) collective-permute-start(bf16[32,4,8]{0,2,1:T(8,128)(2,1)S(1)} %get-tuple-element.302), channel_id=1, source_target_pairs={{0,4},{4,8},{8,12},{12,0},{1,5},{5,9},{9,13},{13,1},{2,6},{6,10},{... | collective-permute-start | bytes 6152 | tf_op jit(solution)/shard_map/while/body/eval_jaxpr/ppermute | solution.py:17
  82.8 8.1 %collective-permute-done.2 = bf16[32,4,8]{0,2,1:T(8,128)(2,1)S(1)} collective-permute-done((bf16[32,4,8]{0,2,1:T(8,128)(2,1)S(1)}, bf16[32,4,8]{0,2,1:T(8,128)(2,1)S(1)}, u32[]{:S(2)}, u32[]{:S(2)}) %collective-permute-start.2) | collective-permute-done | bytes 2080 | tf_op jit(solution)/shard_map/while/body/eval_jaxpr/ppermute | solution.py:17
  91.2 4.4 %bitcast_reduce_fusion.3 = (f32[32,4,8]{0,2,1:T(8,128)S(1)}, f32[4,3072,32,8]{1,2,3,0:T(8,128)S(1)}) fusion(pred[3072]{0:T(1024)(128)(4,1)S(1)} %add_compare_fusion.3, bf16[32,4,8,128]{3,0,2,1:T(8,128)(2,1)S(1)} %copy.133, bf16[3072,4,128,1]{2,1,0,3:T(4,128)(2,1)} %bitcast.100), kind=kOutput, calls=%fused_computation.2.clone.clone.1 | convolution fusion | flops 814742528 | bytes 15997952 | tf_op jit(solution)/shard_map/while/body/eval_jaxpr/rkgd,nkd->rkgn/dot_general | solution.py:40
  95.6 3.6 %fusion.105 = f32[32,4,8]{0,2,1:T(8,128)S(1)} fusion(f32[4,3072,32,8]{1,2,3,0:T(8,128)S(1)} %get-tuple-element.298, f32[32,4,8]{0,2,1:T(8,128)S(1)} %get-tuple-element.299, pred[3072]{0:T(1024)(128)(4,1)S(1)} %add_compare_fusion.3), kind=kLoop, calls=%fused_computation.6.clone.clone.1 | loop fusion | flops 15727616 | bytes 12594176 | tf_op jit(solution)/shard_map/while/body/eval_jaxpr/reduce_sum | solution.py:47
  99.2 5.6 %fusion.107 = bf16[32,4,8,128]{3,0,2,1:T(8,128)(2,1)S(1)} fusion(bf16[3072,4,128,1]{2,1,0,3:T(4,128)(2,1)} %bitcast.101, f32[4,3072,32,8]{1,2,3,0:T(8,128)S(1)} %get-tuple-element.298, f32[32,4,8]{0,2,1:T(8,128)S(1)} %get-tuple-element.299, pred[3072]{0:T(1024)(128)(4,1)S(1)} %add_compare_fusion.3, ...), kind=kOutput, calls=%fused_computation.17.clone.clone.1 | convolution fusion | flops 821690368 | bytes 16530433 | tf_op jit(solution)/shard_map/while/body/eval_jaxpr/rkgn,nkd->rkgd/dot_general | solution.py:48
  105.0 0.6 collective-permute-start.2
  105.6 4.3 %collective-permute-start.3 = (bf16[32,4,8]{0,2,1:T(8,128)(2,1)S(1)}, bf16[32,4,8]{0,2,1:T(8,128)(2,1)S(1)}, u32[]{:S(2)}, u32[]{:S(2)}) collective-permute-start(bf16[32,4,8]{0,2,1:T(8,128)(2,1)S(1)} %get-tuple-element.302), channel_id=1, source_target_pairs={{0,4},{4,8},{8,12},{12,0},{1,5},{5,9},{9,13},{13,1},{2,6},{6,10},{... | collective-permute-start | bytes 6152 | tf_op jit(solution)/shard_map/while/body/eval_jaxpr/ppermute | solution.py:17
  109.9 7.3 %collective-permute-done.2 = bf16[32,4,8]{0,2,1:T(8,128)(2,1)S(1)} collective-permute-done((bf16[32,4,8]{0,2,1:T(8,128)(2,1)S(1)}, bf16[32,4,8]{0,2,1:T(8,128)(2,1)S(1)}, u32[]{:S(2)}, u32[]{:S(2)}) %collective-permute-start.2) | collective-permute-done | bytes 2080 | tf_op jit(solution)/shard_map/while/body/eval_jaxpr/ppermute | solution.py:17
  117.4 4.4 %bitcast_reduce_fusion.3 = (f32[32,4,8]{0,2,1:T(8,128)S(1)}, f32[4,3072,32,8]{1,2,3,0:T(8,128)S(1)}) fusion(pred[3072]{0:T(1024)(128)(4,1)S(1)} %add_compare_fusion.3, bf16[32,4,8,128]{3,0,2,1:T(8,128)(2,1)S(1)} %copy.133, bf16[3072,4,128,1]{2,1,0,3:T(4,128)(2,1)} %bitcast.100), kind=kOutput, calls=%fused_computation.2.clone.clone.1 | convolution fusion | flops 814742528 | bytes 15997952 | tf_op jit(solution)/shard_map/while/body/eval_jaxpr/rkgd,nkd->rkgn/dot_general | solution.py:40
  121.8 3.6 %fusion.105 = f32[32,4,8]{0,2,1:T(8,128)S(1)} fusion(f32[4,3072,32,8]{1,2,3,0:T(8,128)S(1)} %get-tuple-element.298, f32[32,4,8]{0,2,1:T(8,128)S(1)} %get-tuple-element.299, pred[3072]{0:T(1024)(128)(4,1)S(1)} %add_compare_fusion.3), kind=kLoop, calls=%fused_computation.6.clone.clone.1 | loop fusion | flops 15727616 | bytes 12594176 | tf_op jit(solution)/shard_map/while/body/eval_jaxpr/reduce_sum | solution.py:47
  125.4 5.6 %fusion.107 = bf16[32,4,8,128]{3,0,2,1:T(8,128)(2,1)S(1)} fusion(bf16[3072,4,128,1]{2,1,0,3:T(4,128)(2,1)} %bitcast.101, f32[4,3072,32,8]{1,2,3,0:T(8,128)S(1)} %get-tuple-element.298, f32[32,4,8]{0,2,1:T(8,128)S(1)} %get-tuple-element.299, pred[3072]{0:T(1024)(128)(4,1)S(1)} %add_compare_fusion.3, ...), kind=kOutput, calls=%fused_computation.17.clone.clone.1 | convolution fusion | flops 821690368 | bytes 16530433 | tf_op jit(solution)/shard_map/while/body/eval_jaxpr/rkgn,nkd->rkgd/dot_general | solution.py:48
  131.2 0.6 collective-permute-start.2
  131.8 4.3 %collective-permute-start.3 = (bf16[32,4,8]{0,2,1:T(8,128)(2,1)S(1)}, bf16[32,4,8]{0,2,1:T(8,128)(2,1)S(1)}, u32[]{:S(2)}, u32[]{:S(2)}) collective-permute-start(bf16[32,4,8]{0,2,1:T(8,128)(2,1)S(1)} %get-tuple-element.302), channel_id=1, source_target_pairs={{0,4},{4,8},{8,12},{12,0},{1,5},{5,9},{9,13},{13,1},{2,6},{6,10},{... | collective-permute-start | bytes 6152 | tf_op jit(solution)/shard_map/while/body/eval_jaxpr/ppermute | solution.py:17
  136.1 6.4 %collective-permute-done.2 = bf16[32,4,8]{0,2,1:T(8,128)(2,1)S(1)} collective-permute-done((bf16[32,4,8]{0,2,1:T(8,128)(2,1)S(1)}, bf16[32,4,8]{0,2,1:T(8,128)(2,1)S(1)}, u32[]{:S(2)}, u32[]{:S(2)}) %collective-permute-start.2) | collective-permute-done | bytes 2080 | tf_op jit(solution)/shard_map/while/body/eval_jaxpr/ppermute | solution.py:17
  142.7 0.1 copy.76
  142.8 0.1 copy.68
  142.9 1.9 all-gather.1
  144.8 0.1 copy.93
  144.8 0.1 copy.92
  144.9 1.8 all-gather.2
  146.8 0.1 copy.96
  146.9 0.1 copy.97
  147.0 2.2 all-gather
  149.2 0.4 fusion.79
  149.6 0.4 fusion.53
  150.0 1.3 fusion.46
  151.3 0.1 copy.79
  151.5 0.8 copy.120
  152.3 26.3 %all-gather.6.cloned.1.call-done = bf16[128,4096]{1,0:T(8,128)(2,1)} async-done(((bf16[32,4096]{1,0:T(8,128)(2,1)}), bf16[128,4096]{1,0:T(8,128)(2,1)}) %all-gather.6.cloned.1.call-update) | async-done | bytes 1048592 | tf_op jit(solution)/shard_map/all_gather | solution.py:134
  178.7 5.7 %convolution_convert_fusion.1 = bf16[128,1024]{1,0:T(8,128)(2,1)} fusion(bf16[128,4096]{1,0:T(8,128)(2,1)} %all-gather.6.cloned.1.call-done, bf16[4096,1024]{1,0:T(8,128)(2,1)} %param.21), kind=kOutput, calls=%fused_computation.40 | convolution fusion | flops 1073872896 | bytes 9699328 | tf_op jit(solution)/shard_map/dot_general | solution.py:133
  184.4 0.2 reduce-scatter.3.cloned.1.call-start
  184.6 20.5 %copy.100 = bf16[128,8,2,7168]{3,1,2,0:T(8,128)(2,1)} copy(bf16[128,8,2,7168]{3,2,1,0:T(2,128)(2,1)} %bitcast.99) | data formatting | bytes 58720256
  205.2 2.0 all-reduce.2.cloned.1.call-done
  207.2 1.1 fusion.47
  208.3 15.8 %psum.15 = f32[128]{0:T(128)S(1)} all-reduce(f32[128]{0:T(128)S(1)} %get-tuple-element.167), channel_id=1, replica_groups=mesh['groups'=2,'ctx'=4,'kv'=2,'khalf'=2] {'ctx','khalf'}, use_global_device_ids=true, to_apply=%region_8.9 | all-reduce | flops 128 | bytes 1024 | tf_op jit(solution)/shard_map/psum | solution.py:69
  224.2 15.2 %convolution_convert_fusion = bf16[128,14336]{1,0:T(8,128)(2,1)} fusion(bf16[1024,14336]{1,0:T(8,128)(2,1)} %bitcast.98, bf16[128,1024]{1,0:T(8,128)(2,1)S(1)} %get-tuple-element.168, f32[1024]{0:T(1024)S(1)} %copy-done.1, f32[128]{0:T(128)S(1)} %add_rsqrt_fusion), kind=kOutput, calls=%fused_computation.30 | convolution fusion | flops 3760455680 | bytes 33296896 | tf_op jit(solution)/shard_map/dot_general | solution.py:147
  239.4 42.3 %reduce-scatter.3.cloned.1.call-done = bf16[16,14336]{1,0:T(8,128)(2,1)} async-done(((bf16[128,14336]{1,0:T(8,128)(2,1)}), bf16[16,14336]{1,0:T(8,128)(2,1)}) %reduce-scatter.3.cloned.1.call-update) | async-done | bytes 458768 | tf_op jit(solution)/shard_map/reduce_scatter | solution.py:146
  281.8 1.1 convert_element_type.179
  282.8 0.8 fusion.52
  283.7 25.5 %all-gather.8.cloned.1.call-done = bf16[128,7168]{1,0:T(8,128)(2,1)} async-done(((bf16[16,7168]{1,0:T(8,128)(2,1)}), bf16[128,7168]{1,0:T(8,128)(2,1)}) %all-gather.8.cloned.1.call-update) | async-done | bytes 1835024 | tf_op jit(solution)/shard_map/all_gather | solution.py:154
  309.2 8.5 %convolution_convert_fusion.2 = bf16[128,1024]{1,0:T(8,128)(2,1)} fusion(bf16[128,7168]{1,0:T(8,128)(2,1)} %all-gather.8.cloned.1.call-done, bf16[7168,1024]{1,0:T(8,128)(2,1)} %param.23), kind=kOutput, calls=%fused_computation.42 | convolution fusion | flops 1879179264 | bytes 16777216 | tf_op jit(solution)/shard_map/dot_general | solution.py:153
  317.8 11.3 %reduce-scatter.5.cloned.1.call-done = bf16[64,1024]{1,0:T(8,128)(2,1)} async-done(((bf16[128,1024]{1,0:T(8,128)(2,1)}), bf16[64,1024]{1,0:T(8,128)(2,1)}) %reduce-scatter.5.cloned.1.call-update) | async-done | bytes 131088 | tf_op jit(solution)/shard_map/reduce_scatter | solution.py:158
  329.1 1.6 add_convert_fusion.1
  (72 shorter events, 1.6 us)
Async XLA Ops:
  6.5 172.1 %all-gather.6.cloned.1.call-start = ((), (), s32[]{:S(2)}) async-start(), calls=%async_computation.2 | async-start | bytes 1310720 | tf_op jit(solution)/shard_map/all_gather | solution.py:134
  49.8 14.2 %collective-permute-start.1 = (bf16[32,4,8,128]{3,0,2,1:T(8,128)(2,1)S(1)}, bf16[32,4,8,128]{3,0,2,1:T(8,128)(2,1)S(1)}, u32[]{:S(2)}, u32[]{:S(2)}) collective-permute-start(bf16[32,4,8,128]{3,0,2,1:T(8,128)(2,1)S(1)} %fusion.107), channel_id=1, source_target_pairs={{0,4},{4,8},{8,12},{12,0},{1,5},{5,9},{9,13},{13,1},{2,6},{6,10},{... | collective-permute-start | bytes 786440 | tf_op jit(solution)/shard_map/while/body/eval_jaxpr/ppermute | solution.py:17
  51.9 12.2 %collective-permute-start = (bf16[32,4,8,128]{3,0,2,1:T(8,128)(2,1)S(1)}, bf16[32,4,8,128]{3,0,2,1:T(8,128)(2,1)S(1)}, u32[]{:S(2)}, u32[]{:S(2)}) collective-permute-start(bf16[32,4,8,128]{3,0,2,1:T(8,128)(2,1)S(1)} %copy.133), channel_id=1, source_target_pairs={{0,4},{4,8},{8,12},{12,0},{1,5},{5,9},{9,13},{13,1},{2,6},{6,10},{... | collective-permute-start | bytes 786440 | tf_op jit(solution)/shard_map/while/body/eval_jaxpr/ppermute | solution.py:17
  52.0 11.9 %collective-permute-start.2 = (bf16[32,4,8]{0,2,1:T(8,128)(2,1)S(1)}, bf16[32,4,8]{0,2,1:T(8,128)(2,1)S(1)}, u32[]{:S(2)}, u32[]{:S(2)}) collective-permute-start(bf16[32,4,8]{0,2,1:T(8,128)(2,1)S(1)} %fusion.108), channel_id=1, source_target_pairs={{0,4},{4,8},{8,12},{12,0},{1,5},{5,9},{9,13},{13,1},{2,6},{6,10},{... | collective-permute-start | bytes 6152 | tf_op jit(solution)/shard_map/while/body/eval_jaxpr/ppermute | solution.py:17
  54.9 9.1 %collective-permute-start.3 = (bf16[32,4,8]{0,2,1:T(8,128)(2,1)S(1)}, bf16[32,4,8]{0,2,1:T(8,128)(2,1)S(1)}, u32[]{:S(2)}, u32[]{:S(2)}) collective-permute-start(bf16[32,4,8]{0,2,1:T(8,128)(2,1)S(1)} %get-tuple-element.302), channel_id=1, source_target_pairs={{0,4},{4,8},{8,12},{12,0},{1,5},{5,9},{9,13},{13,1},{2,6},{6,10},{... | collective-permute-start | bytes 6152 | tf_op jit(solution)/shard_map/while/body/eval_jaxpr/ppermute | solution.py:17
  77.8 13.2 %collective-permute-start.1 = (bf16[32,4,8,128]{3,0,2,1:T(8,128)(2,1)S(1)}, bf16[32,4,8,128]{3,0,2,1:T(8,128)(2,1)S(1)}, u32[]{:S(2)}, u32[]{:S(2)}) collective-permute-start(bf16[32,4,8,128]{3,0,2,1:T(8,128)(2,1)S(1)} %fusion.107), channel_id=1, source_target_pairs={{0,4},{4,8},{8,12},{12,0},{1,5},{5,9},{9,13},{13,1},{2,6},{6,10},{... | collective-permute-start | bytes 786440 | tf_op jit(solution)/shard_map/while/body/eval_jaxpr/ppermute | solution.py:17
  77.9 13.2 %collective-permute-start = (bf16[32,4,8,128]{3,0,2,1:T(8,128)(2,1)S(1)}, bf16[32,4,8,128]{3,0,2,1:T(8,128)(2,1)S(1)}, u32[]{:S(2)}, u32[]{:S(2)}) collective-permute-start(bf16[32,4,8,128]{3,0,2,1:T(8,128)(2,1)S(1)} %copy.133), channel_id=1, source_target_pairs={{0,4},{4,8},{8,12},{12,0},{1,5},{5,9},{9,13},{13,1},{2,6},{6,10},{... | collective-permute-start | bytes 786440 | tf_op jit(solution)/shard_map/while/body/eval_jaxpr/ppermute | solution.py:17
  78.0 13.0 %collective-permute-start.2 = (bf16[32,4,8]{0,2,1:T(8,128)(2,1)S(1)}, bf16[32,4,8]{0,2,1:T(8,128)(2,1)S(1)}, u32[]{:S(2)}, u32[]{:S(2)}) collective-permute-start(bf16[32,4,8]{0,2,1:T(8,128)(2,1)S(1)} %fusion.108), channel_id=1, source_target_pairs={{0,4},{4,8},{8,12},{12,0},{1,5},{5,9},{9,13},{13,1},{2,6},{6,10},{... | collective-permute-start | bytes 6152 | tf_op jit(solution)/shard_map/while/body/eval_jaxpr/ppermute | solution.py:17
  79.3 11.7 %collective-permute-start.3 = (bf16[32,4,8]{0,2,1:T(8,128)(2,1)S(1)}, bf16[32,4,8]{0,2,1:T(8,128)(2,1)S(1)}, u32[]{:S(2)}, u32[]{:S(2)}) collective-permute-start(bf16[32,4,8]{0,2,1:T(8,128)(2,1)S(1)} %get-tuple-element.302), channel_id=1, source_target_pairs={{0,4},{4,8},{8,12},{12,0},{1,5},{5,9},{9,13},{13,1},{2,6},{6,10},{... | collective-permute-start | bytes 6152 | tf_op jit(solution)/shard_map/while/body/eval_jaxpr/ppermute | solution.py:17
  104.9 12.4 %collective-permute-start.1 = (bf16[32,4,8,128]{3,0,2,1:T(8,128)(2,1)S(1)}, bf16[32,4,8,128]{3,0,2,1:T(8,128)(2,1)S(1)}, u32[]{:S(2)}, u32[]{:S(2)}) collective-permute-start(bf16[32,4,8,128]{3,0,2,1:T(8,128)(2,1)S(1)} %fusion.107), channel_id=1, source_target_pairs={{0,4},{4,8},{8,12},{12,0},{1,5},{5,9},{9,13},{13,1},{2,6},{6,10},{... | collective-permute-start | bytes 786440 | tf_op jit(solution)/shard_map/while/body/eval_jaxpr/ppermute | solution.py:17
  104.9 12.4 %collective-permute-start = (bf16[32,4,8,128]{3,0,2,1:T(8,128)(2,1)S(1)}, bf16[32,4,8,128]{3,0,2,1:T(8,128)(2,1)S(1)}, u32[]{:S(2)}, u32[]{:S(2)}) collective-permute-start(bf16[32,4,8,128]{3,0,2,1:T(8,128)(2,1)S(1)} %copy.133), channel_id=1, source_target_pairs={{0,4},{4,8},{8,12},{12,0},{1,5},{5,9},{9,13},{13,1},{2,6},{6,10},{... | collective-permute-start | bytes 786440 | tf_op jit(solution)/shard_map/while/body/eval_jaxpr/ppermute | solution.py:17
  105.0 12.1 %collective-permute-start.2 = (bf16[32,4,8]{0,2,1:T(8,128)(2,1)S(1)}, bf16[32,4,8]{0,2,1:T(8,128)(2,1)S(1)}, u32[]{:S(2)}, u32[]{:S(2)}) collective-permute-start(bf16[32,4,8]{0,2,1:T(8,128)(2,1)S(1)} %fusion.108), channel_id=1, source_target_pairs={{0,4},{4,8},{8,12},{12,0},{1,5},{5,9},{9,13},{13,1},{2,6},{6,10},{... | collective-permute-start | bytes 6152 | tf_op jit(solution)/shard_map/while/body/eval_jaxpr/ppermute | solution.py:17
  105.6 11.6 %collective-permute-start.3 = (bf16[32,4,8]{0,2,1:T(8,128)(2,1)S(1)}, bf16[32,4,8]{0,2,1:T(8,128)(2,1)S(1)}, u32[]{:S(2)}, u32[]{:S(2)}) collective-permute-start(bf16[32,4,8]{0,2,1:T(8,128)(2,1)S(1)} %get-tuple-element.302), channel_id=1, source_target_pairs={{0,4},{4,8},{8,12},{12,0},{1,5},{5,9},{9,13},{13,1},{2,6},{6,10},{... | collective-permute-start | bytes 6152 | tf_op jit(solution)/shard_map/while/body/eval_jaxpr/ppermute | solution.py:17
  131.0 11.5 %collective-permute-start.1 = (bf16[32,4,8,128]{3,0,2,1:T(8,128)(2,1)S(1)}, bf16[32,4,8,128]{3,0,2,1:T(8,128)(2,1)S(1)}, u32[]{:S(2)}, u32[]{:S(2)}) collective-permute-start(bf16[32,4,8,128]{3,0,2,1:T(8,128)(2,1)S(1)} %fusion.107), channel_id=1, source_target_pairs={{0,4},{4,8},{8,12},{12,0},{1,5},{5,9},{9,13},{13,1},{2,6},{6,10},{... | collective-permute-start | bytes 786440 | tf_op jit(solution)/shard_map/while/body/eval_jaxpr/ppermute | solution.py:17
  131.1 11.5 %collective-permute-start = (bf16[32,4,8,128]{3,0,2,1:T(8,128)(2,1)S(1)}, bf16[32,4,8,128]{3,0,2,1:T(8,128)(2,1)S(1)}, u32[]{:S(2)}, u32[]{:S(2)}) collective-permute-start(bf16[32,4,8,128]{3,0,2,1:T(8,128)(2,1)S(1)} %copy.133), channel_id=1, source_target_pairs={{0,4},{4,8},{8,12},{12,0},{1,5},{5,9},{9,13},{13,1},{2,6},{6,10},{... | collective-permute-start | bytes 786440 | tf_op jit(solution)/shard_map/while/body/eval_jaxpr/ppermute | solution.py:17
  131.2 11.3 %collective-permute-start.2 = (bf16[32,4,8]{0,2,1:T(8,128)(2,1)S(1)}, bf16[32,4,8]{0,2,1:T(8,128)(2,1)S(1)}, u32[]{:S(2)}, u32[]{:S(2)}) collective-permute-start(bf16[32,4,8]{0,2,1:T(8,128)(2,1)S(1)} %fusion.108), channel_id=1, source_target_pairs={{0,4},{4,8},{8,12},{12,0},{1,5},{5,9},{9,13},{13,1},{2,6},{6,10},{... | collective-permute-start | bytes 6152 | tf_op jit(solution)/shard_map/while/body/eval_jaxpr/ppermute | solution.py:17
  131.8 10.8 %collective-permute-start.3 = (bf16[32,4,8]{0,2,1:T(8,128)(2,1)S(1)}, bf16[32,4,8]{0,2,1:T(8,128)(2,1)S(1)}, u32[]{:S(2)}, u32[]{:S(2)}) collective-permute-start(bf16[32,4,8]{0,2,1:T(8,128)(2,1)S(1)} %get-tuple-element.302), channel_id=1, source_target_pairs={{0,4},{4,8},{8,12},{12,0},{1,5},{5,9},{9,13},{13,1},{2,6},{6,10},{... | collective-permute-start | bytes 6152 | tf_op jit(solution)/shard_map/while/body/eval_jaxpr/ppermute | solution.py:17
  152.3 54.9 %all-reduce.2.cloned.1.call-start = ((), (), s32[]{:S(2)}) async-start(), calls=%async_computation.3 | async-start | bytes 524288 | tf_op jit(solution)/shard_map/psum | solution.py:138
  184.4 97.4 %reduce-scatter.3.cloned.1.call-start = ((), (), s32[]{:S(2)}) async-start(), calls=%async_computation.4 | async-start | bytes 4128768 | tf_op jit(solution)/shard_map/reduce_scatter | solution.py:146
  184.6 22.6 %copy-start = (bf16[128,1024]{1,0:T(8,128)(2,1)S(1)}, bf16[128,1024]{1,0:T(8,128)(2,1)}, u32[]{:S(2)}) copy-start(bf16[128,1024]{1,0:T(8,128)(2,1)} %param.19) | copy-start | bytes 786436
  184.6 39.6 %copy-start.1 = (f32[1024]{0:T(1024)S(1)}, f32[1024]{0:T(1024)}, u32[]{:S(2)}) copy-start(f32[1024]{0:T(1024)} %param.20) | copy-start | bytes 12292
  239.4 69.8 %all-gather.8.cloned.1.call-start = ((), (), s32[]{:S(2)}) async-start(), calls=%async_computation.5 | async-start | bytes 2064384 | tf_op jit(solution)/shard_map/all_gather | solution.py:154
  283.7 45.4 %reduce-scatter.5.cloned.1.call-start = ((), (), s32[]{:S(2)}) async-start(), calls=%async_computation.6 | async-start | bytes 393216 | tf_op jit(solution)/shard_map/reduce_scatter | solution.py:158
Sparse Core Ops, SparseCore 0:
  152.4 26.2 all-gather.5
  184.5 22.6 all-reduce.1
  239.5 42.2 reduce-scatter.2
  283.8 25.3 all-gather.7
  317.9 11.1 reduce-scatter.4
